TPU v7x, 32 devices: a whole 2x2x4 slice. The times are simulated.
32 devices in a mesh: dp: 8 (over y, x, core), tensor: 4 (over z).
Axes of the slice: x: 2, y: 2, z: 4, core: 2. Of those that a mesh axis runs over, the one named last changes fastest.
Arguments:
- tokens: bfloat16 [16384, 2048], P(('dp', 'tensor'))
- teacher: bfloat16 [16384, 2048], P(('dp', 'tensor')), may hold values from -6 to 6
- valid: int32 [16384], P(('dp', 'tensor')), may hold values from 0 to 1, as said below
- prefix: int32 [16], P('dp'), may hold values from 102 to 512, as said below
- w_query: bfloat16 [2048, 1024], P(None, 'tensor'), may hold values from -0.125 to 0.125
- key_weight: bfloat16 [2048, 256], replicated, may hold values from -0.125 to 0.125
- value_weight: bfloat16 [2048, 256], replicated, may hold values from -0.125 to 0.125
- query_gain: float32 [64], replicated, may hold values from 0.25 to 1.75
- key_gain: float32 [64], replicated, may hold values from 0.25 to 1.75
- w_out: bfloat16 [1024, 2048], P('tensor'), may hold values from -3 to 3
- attn_gain: float32 [2048], replicated, may hold values from 0.25 to 1.75
- ffn_gain: float32 [2048], replicated, may hold values from 0.25 to 1.75
- w_gate: bfloat16 [2048, 5120], P(None, 'tensor'), may hold values from -0.125 to 0.125
- w_up: bfloat16 [2048, 5120], P(None, 'tensor'), may hold values from -0.125 to 0.125
- w_down: bfloat16 [5120, 2048], P('tensor'), may hold values from -0.078125 to 0.078125
Outputs:
- output: bfloat16 [16384, 2048], P(('dp', 'tensor'))
- loss: float32 [], replicated
- grad_tokens: float32 [16384, 2048], P(('dp', 'tensor'))
- grad_query: float32 [2048, 1024], P(None, 'tensor')
- grad_key: float32 [2048, 256], replicated
- grad_value: float32 [2048, 256], replicated
- grad_query_gain: float32 [64], replicated
- grad_key_gain: float32 [64], replicated
- grad_out: float32 [1024, 2048], P('tensor')
- grad_attn_gain: float32 [2048], replicated
- grad_ffn_gain: float32 [2048], replicated
- grad_gate: float32 [2048, 5120], P(None, 'tensor')
- grad_up: float32 [2048, 5120], P(None, 'tensor')
- grad_down: float32 [5120, 2048], P('tensor')
Inputs may be any that keep to these rules, and one draw needn't show every extreme that they name: The first token of every sequence is valid. One sequence has prefix length exactly 512 and another exactly 102.
All inputs are finite; a program needn't handle non-finite values.
Results may differ from a plain program's by a relative error of at most 0.015.
Values may be sent and summed in bfloat16 or wider, within the bound.
A program may use at most 256 MiB of HBM per device.

v0:
```python
import jax
import jax.numpy as jnp
from jax import lax
from jax.sharding import PartitionSpec as P

QUERY_HEADS = 16
KEY_VALUE_HEADS = 4
HEAD_SIZE = 64
SEQ_LEN = 1024


EPSILON = 1e-06


def rope_tables(sequence_length, head_size):
    half_size = head_size // 2
    frequency = 10000.0 ** (-2.0 * jnp.arange(half_size, dtype=jnp.float32) / head_size)
    angles = jnp.arange(sequence_length, dtype=jnp.float32)[:, None] * frequency[None, :]
    cosine = jnp.concatenate([jnp.cos(angles), jnp.cos(angles)], 1)
    sine_tab = jnp.concatenate([jnp.sin(angles), jnp.sin(angles)], 1)
    return (cosine, sine_tab)


def rotate(vector, cosine, sine_tab):
    half_size = vector.shape[-1] // 2
    turned = jnp.concatenate([-vector[..., half_size:], vector[..., :half_size]], -1)
    return vector * cosine + turned * sine_tab


def unrotate(gradient, cosine, sine_tab):
    half_size = gradient.shape[-1] // 2
    shifted = gradient * sine_tab
    return gradient * cosine + jnp.concatenate(
        [shifted[..., half_size:], -shifted[..., :half_size]], -1
    )


def inv_root(vector):
    return lax.rsqrt(jnp.mean(vector * vector, axis=-1, keepdims=True) + EPSILON)


def norm_back(gradient, source, factor, gain_vec):
    scaled = gradient * gain_vec
    return factor * scaled - source * factor**3 * jnp.mean(scaled * source, axis=-1, keepdims=True)


def visible(sequence_length, prefix_len):
    row_pos = jnp.arange(sequence_length)[:, None]
    col_pos = jnp.arange(sequence_length)[None, :]
    return (col_pos <= row_pos) | (row_pos < prefix_len) & (col_pos < prefix_len)


def attend(query_matrix, key_matrix, value_matrix, prefix_len, kv_dev):
    sequence_length, head_count, head_size = query_matrix.shape
    grouped_heads = query_matrix.reshape(sequence_length, kv_dev, head_count // kv_dev, head_size)
    scores = jnp.einsum(
        "ikgd,jkd->kgij", grouped_heads, key_matrix, preferred_element_type=jnp.float32
    ) * head_size ** (-0.5)
    allowed = visible(sequence_length, prefix_len)
    scores = jnp.where(allowed, scores, -1e30)
    row_max = jnp.max(scores, -1, keepdims=True)
    weights = jnp.where(allowed, jnp.exp(scores - row_max), 0.0)
    row_total = jnp.sum(weights, -1, keepdims=True)
    attn_probs = (weights / row_total).astype(jnp.bfloat16)
    attended = jnp.einsum(
        "kgij,jkd->ikgd", attn_probs, value_matrix, preferred_element_type=jnp.float32
    )
    return (
        attended.reshape(sequence_length, head_count * head_size),
        (row_max + jnp.log(row_total))[..., 0],
    )


def attend_back(query_matrix, key_matrix, value_matrix, prefix_len, summit, grad_attended, kv_dev):
    sequence_length, head_count, head_size = query_matrix.shape
    per_group = head_count // kv_dev
    score_scale = head_size ** (-0.5)
    grouped_heads = query_matrix.reshape(sequence_length, kv_dev, per_group, head_size)
    scores = (
        jnp.einsum("ikgd,jkd->kgij", grouped_heads, key_matrix, preferred_element_type=jnp.float32)
        * score_scale
    )
    allowed = visible(sequence_length, prefix_len)
    attn_probs = jnp.where(
        allowed, jnp.exp(jnp.where(allowed, scores, -1e30) - summit[..., None]), 0.0
    )
    grad_heads = grad_attended.reshape(sequence_length, kv_dev, per_group, head_size)
    grad_probs = jnp.einsum(
        "ikgd,jkd->kgij", grad_heads, value_matrix, preferred_element_type=jnp.float32
    )
    inner_sum = jnp.sum(attn_probs * grad_probs, -1, keepdims=True)
    grad_scores = (attn_probs * (grad_probs - inner_sum)).astype(jnp.bfloat16)
    grad_query = (
        jnp.einsum("kgij,jkd->ikgd", grad_scores, key_matrix, preferred_element_type=jnp.float32)
        * score_scale
    )
    grad_key = (
        jnp.einsum("kgij,ikgd->jkd", grad_scores, grouped_heads, preferred_element_type=jnp.float32)
        * score_scale
    )
    grad_value = jnp.einsum(
        "kgij,ikgd->jkd",
        attn_probs.astype(jnp.bfloat16),
        grad_heads,
        preferred_element_type=jnp.float32,
    )
    return (grad_query.reshape(sequence_length, head_count, head_size), grad_key, grad_value)


def body(
    tokens,
    teacher,
    valid,
    prefix,
    w_query,
    key_weight,
    value_weight,
    query_gain,
    key_gain,
    w_out,
    attn_gain,
    ffn_gain,
    w_gate,
    w_up,
    w_down,
):
    rows_dev, width = tokens.shape
    seq_count = prefix.shape[0]
    sequence_length = SEQ_LEN
    group_rows = seq_count * sequence_length
    heads_dev = w_query.shape[1] // HEAD_SIZE
    queries_per_group = QUERY_HEADS // KEY_VALUE_HEADS
    kv_dev = max(1, heads_dev // queries_per_group)
    query_cols = heads_dev * HEAD_SIZE
    kv_cols = kv_dev * HEAD_SIZE
    kv_start = lax.axis_index("tensor") * heads_dev // queries_per_group * HEAD_SIZE
    key_local = lax.dynamic_slice_in_dim(key_weight, kv_start, kv_cols, 1)
    value_local = lax.dynamic_slice_in_dim(value_weight, kv_start, kv_cols, 1)
    source = tokens.astype(jnp.float32)
    factor_one = inv_root(source)
    normed_input = (source * factor_one * attn_gain).astype(jnp.bfloat16)
    normed_all = lax.all_gather(normed_input, "tensor", axis=0, tiled=True)
    proj_weight = jnp.concatenate([w_query, key_local, value_local], 1)
    projected = jnp.dot(normed_all, proj_weight, preferred_element_type=jnp.float32)
    query_raw = projected[:, :query_cols].reshape(group_rows, heads_dev, HEAD_SIZE)
    key_raw = projected[:, query_cols : query_cols + kv_cols].reshape(group_rows, kv_dev, HEAD_SIZE)
    value_low = (
        projected[:, query_cols + kv_cols :]
        .astype(jnp.bfloat16)
        .reshape(seq_count, sequence_length, kv_dev, HEAD_SIZE)
    )
    query_factor = inv_root(query_raw)
    key_factor = inv_root(key_raw)
    cosine, sine_tab = rope_tables(sequence_length, HEAD_SIZE)
    cos_rows = jnp.tile(cosine, (seq_count, 1))[:, None, :]
    sin_rows = jnp.tile(sine_tab, (seq_count, 1))[:, None, :]
    query_low = (
        rotate(query_raw * query_factor * query_gain, cos_rows, sin_rows)
        .astype(jnp.bfloat16)
        .reshape(seq_count, sequence_length, heads_dev, HEAD_SIZE)
    )
    key_low = (
        rotate(key_raw * key_factor * key_gain, cos_rows, sin_rows)
        .astype(jnp.bfloat16)
        .reshape(seq_count, sequence_length, kv_dev, HEAD_SIZE)
    )
    attended, summit = lax.map(
        lambda packed: attend(packed[0], packed[1], packed[2], packed[3], kv_dev),
        (query_low, key_low, value_low, prefix),
    )
    attended_low = attended.reshape(group_rows, query_cols).astype(jnp.bfloat16)
    middle = source + lax.psum_scatter(
        jnp.dot(attended_low, w_out, preferred_element_type=jnp.float32),
        "tensor",
        scatter_dimension=0,
        tiled=True,
    )
    factor_two = inv_root(middle)
    normed_two = (middle * factor_two * ffn_gain).astype(jnp.bfloat16)
    normed_two_all = lax.all_gather(normed_two, "tensor", axis=0, tiled=True)
    gate_act = jnp.dot(normed_two_all, w_gate, preferred_element_type=jnp.float32)
    up_act = jnp.dot(normed_two_all, w_up, preferred_element_type=jnp.float32)
    sig_gate = jax.nn.sigmoid(gate_act)
    hidden = (gate_act * sig_gate * up_act).astype(jnp.bfloat16)
    result = middle + lax.psum_scatter(
        jnp.dot(hidden, w_down, preferred_element_type=jnp.float32).astype(jnp.bfloat16),
        "tensor",
        scatter_dimension=0,
        tiled=True,
    ).astype(jnp.float32)
    mask_rows = valid.astype(jnp.float32)[:, None]
    error_rows = result - teacher.astype(jnp.float32)
    total_count, total_square = lax.psum(
        (jnp.sum(valid).astype(jnp.float32), jnp.sum(error_rows * error_rows * mask_rows)),
        ("dp", "tensor"),
    )
    loss = total_square / (total_count * width)
    cotangent = group_rows * lax.axis_size("dp") / total_count * error_rows * mask_rows
    cot_all = lax.all_gather(cotangent.astype(jnp.bfloat16), "tensor", axis=0, tiled=True)
    grad_down = jnp.einsum("tf,td->fd", hidden, cot_all, preferred_element_type=jnp.float32)
    grad_hidden = jnp.einsum("td,fd->tf", cot_all, w_down, preferred_element_type=jnp.float32)
    grad_gate_low = (grad_hidden * up_act * sig_gate * (1.0 + gate_act * (1.0 - sig_gate))).astype(
        jnp.bfloat16
    )
    grad_up_low = (grad_hidden * gate_act * sig_gate).astype(jnp.bfloat16)
    gate_part = grad_gate_low
    up_part = grad_up_low
    grad_normed_two = lax.psum_scatter(
        (
            jnp.einsum("tf,df->td", gate_part, w_gate, preferred_element_type=jnp.float32)
            + jnp.einsum("tf,df->td", up_part, w_up, preferred_element_type=jnp.float32)
        ).astype(jnp.bfloat16),
        "tensor",
        scatter_dimension=0,
        tiled=True,
    ).astype(jnp.float32)
    grad_ffn_gain = jnp.sum(grad_normed_two * middle * factor_two, 0)
    grad_middle = cotangent + norm_back(grad_normed_two, middle, factor_two, ffn_gain)
    grad_branch_all = lax.all_gather(grad_middle.astype(jnp.bfloat16), "tensor", axis=0, tiled=True)
    grad_out = jnp.einsum(
        "tq,td->qd", attended_low, grad_branch_all, preferred_element_type=jnp.float32
    )
    grad_attended = jnp.einsum(
        "td,qd->tq", grad_branch_all, w_out, preferred_element_type=jnp.float32
    ).astype(jnp.bfloat16)
    grad_q_rot, grad_k_rot, grad_v = lax.map(
        lambda packed: attend_back(
            packed[0], packed[1], packed[2], packed[3], packed[4], packed[5], kv_dev
        ),
        (
            query_low,
            key_low,
            value_low,
            prefix,
            summit,
            grad_attended.reshape(seq_count, sequence_length, query_cols),
        ),
    )
    grad_k_rot = grad_k_rot.reshape(group_rows, kv_dev, HEAD_SIZE)
    grad_v = grad_v.reshape(group_rows, kv_cols)
    grad_q_normed = unrotate(
        grad_q_rot.reshape(group_rows, heads_dev, HEAD_SIZE), cos_rows, sin_rows
    )
    grad_k_normed = unrotate(grad_k_rot, cos_rows, sin_rows)
    grad_query_gain = jnp.sum(grad_q_normed * query_raw * query_factor, (0, 1))
    grad_key_gain = jnp.sum(grad_k_normed * key_raw * key_factor, (0, 1))
    grad_q_raw = norm_back(grad_q_normed, query_raw, query_factor, query_gain)
    grad_k_raw = norm_back(grad_k_normed, key_raw, key_factor, key_gain)
    back_rows = jnp.concatenate(
        [
            grad_q_raw.reshape(group_rows, query_cols),
            grad_k_raw.reshape(group_rows, kv_cols),
            grad_v,
        ],
        1,
    ).astype(jnp.bfloat16)
    grad_normed = lax.psum_scatter(
        jnp.einsum("tc,dc->td", back_rows, proj_weight, preferred_element_type=jnp.float32).astype(
            jnp.bfloat16
        ),
        "tensor",
        scatter_dimension=0,
        tiled=True,
    ).astype(jnp.float32)
    grad_attn_gain = jnp.sum(grad_normed * source * factor_one, 0)
    grad_tokens = grad_middle + norm_back(grad_normed, source, factor_one, attn_gain)
    grad_proj = jnp.einsum(
        "td,tc->dc",
        lax.all_gather(normed_input, "tensor", axis=0, tiled=True),
        back_rows,
        preferred_element_type=jnp.float32,
    )
    shard_rows = lax.all_gather(normed_two, "tensor", axis=0, tiled=True)
    gate_part = grad_gate_low
    up_part = grad_up_low
    grad_gate = jnp.einsum("td,tf->df", shard_rows, gate_part, preferred_element_type=jnp.float32)
    grad_up = jnp.einsum("td,tf->df", shard_rows, up_part, preferred_element_type=jnp.float32)
    grad_query = grad_proj[:, :query_cols]
    zero_kv = jnp.zeros((width, key_weight.shape[1]), jnp.float32)
    key_full = lax.dynamic_update_slice_in_dim(
        zero_kv, grad_proj[:, query_cols : query_cols + kv_cols], kv_start, 1
    )
    value_full = lax.dynamic_update_slice_in_dim(
        zero_kv, grad_proj[:, query_cols + kv_cols :], kv_start, 1
    )
    grad_query, grad_out, grad_gate, grad_up, grad_down = (
        lax.psum(grad_query.astype(jnp.bfloat16), "dp").astype(jnp.float32),
        lax.psum(grad_out.astype(jnp.bfloat16), "dp").astype(jnp.float32),
        lax.psum(grad_gate.astype(jnp.bfloat16), "dp").astype(jnp.float32),
        lax.psum(grad_up.astype(jnp.bfloat16), "dp").astype(jnp.float32),
        lax.psum(grad_down.astype(jnp.bfloat16), "dp").astype(jnp.float32),
    )
    key_full, value_full, grad_query_gain, grad_key_gain, grad_attn_gain, grad_ffn_gain = lax.psum(
        (key_full, value_full, grad_query_gain, grad_key_gain, grad_attn_gain, grad_ffn_gain),
        ("dp", "tensor"),
    )
    return (
        result.astype(jnp.bfloat16),
        loss,
        grad_tokens,
        grad_query,
        key_full,
        value_full,
        grad_query_gain,
        grad_key_gain,
        grad_out,
        grad_attn_gain,
        grad_ffn_gain,
        grad_gate,
        grad_up,
        grad_down,
    )


def solution(mesh):
    placed = (
        P(("dp", "tensor"), None),
        P(("dp", "tensor"), None),
        P(("dp", "tensor")),
        P("dp"),
        P(None, "tensor"),
        P(),
        P(),
        P(),
        P(),
        P("tensor", None),
        P(),
        P(),
        P(None, "tensor"),
        P(None, "tensor"),
        P("tensor", None),
    )
    return jax.shard_map(
        body,
        mesh=mesh,
        in_specs=placed,
        out_specs=(
            P(("dp", "tensor"), None),
            P(),
            P(("dp", "tensor"), None),
            P(None, "tensor"),
            P(),
            P(),
            P(),
            P(),
            P("tensor", None),
            P(),
            P(),
            P(None, "tensor"),
            P(None, "tensor"),
            P("tensor", None),
        ),
        check_vma=False,
    )
```

profile of v0, /device:TPU:0, one launch (start us, length us, event | category | flops | bytes accessed | tf_op | source)
XLA Modules:
  0.0 2096.2 jit_solution(9297197625935668544)
XLA Ops:
  10.5 3.5 fusion.64
  17.7 148.8 %all-gather.5.cloned.1.call-done = bf16[2048,2048]{1,0:T(8,128)(2,1)} async-done(((bf16[512,2048]{1,0:T(8,128)(2,1)}), bf16[2048,2048]{1,0:T(8,128)(2,1)}) %all-gather.5.cloned.1.call-update) | async-done | bytes 8388624 | tf_op jit(solution)/shard_map/all_gather | solution.py:142
  166.5 7.3 fusion.80
  183.8 3.1 concatenate.48
  186.9 3.1 concatenate.49
  192.7 3.7 fusion.75
  196.8 34.6 %while.26 = (s32[]{:T(128)}, bf16[2,1024,256]{2,1,0:T(8,128)(2,1)}, f32[2,1,4,1024]{3,2,1,0:T(4,128)}, bf16[2,1024,1,64]{1,3,2,0:T(8,128)(2,1)S(1)}, s32[2]{0:T(...) while((s32[]{:T(128)}, bf16[2,1024,256]{2,1,0:T(8,128)(2,1)}, ...), condition=%wide.region_6.7_spmd, body=%wide.region_3.6_spmd.sunk | while | flops 1135604736 | bytes 58068088 | solution.py:167
  198.8 3.9 fusion.150
  202.7 4.2 fusion.151
  206.9 5.6 fusion.152
  216.0 3.9 fusion.150
  219.9 4.2 fusion.151
  224.1 5.6 fusion.152
  231.4 9.8 fusion.93
  241.3 278.6 %reduce-scatter.5.cloned.1.call-done = f32[512,2048]{1,0:T(8,128)} async-done(((f32[2048,2048]{1,0:T(8,128)}), f32[512,2048]{1,0:T(8,128)}) %reduce-scatter.5.cloned.1.call-update) | async-done | bytes 4194320 | tf_op jit(solution)/shard_map/reduce_scatter | solution.py:172
  520.0 4.7 multiply_reduce_fusion.1
  525.9 3.9 multiply_convert_fusion.3
  529.8 150.5 %all-gather.7.cloned.1.call-done = bf16[2048,2048]{1,0:T(8,128)(2,1)} async-done(((bf16[512,2048]{1,0:T(8,128)(2,1)}), bf16[2048,2048]{1,0:T(8,128)(2,1)}) %all-gather.7.cloned.1.call-update) | async-done | bytes 8388624 | tf_op jit(solution)/shard_map/all_gather | solution.py:180
  680.3 16.9 fusion.94
  697.2 17.2 multiply_convert_fusion.2
  714.4 16.6 convolution_convert_fusion.1
  733.0 43.1 %psum.92 = f32[]{:T(128)} all-reduce(f32[]{:T(128)S(6)} %convert_element_type.123), channel_id=1, replica_groups=mesh['dp'=8,'tensor'=4] {'dp','tensor'}, use_global_device_ids=true, to_apply=%region_13.14 | all-reduce | flops 1 | bytes 8 | tf_op jit(solution)/shard_map/psum | solution.py:193
  776.7 98.1 %reduce-scatter.7.cloned.1.call-done = bf16[512,2048]{1,0:T(8,128)(2,1)} async-done(((bf16[2048,2048]{1,0:T(8,128)(2,1)}), bf16[512,2048]{1,0:T(8,128)(2,1)}) %reduce-scatter.7.cloned.1.call-update) | async-done | bytes 2097168 | tf_op jit(solution)/shard_map/reduce_scatter | solution.py:185
  874.9 5.4 fusion.69
  880.4 150.5 %all-gather.9.cloned.1.call-done = bf16[2048,2048]{1,0:T(8,128)(2,1)} async-done(((bf16[512,2048]{1,0:T(8,128)(2,1)}), bf16[2048,2048]{1,0:T(8,128)(2,1)}) %all-gather.9.cloned.1.call-update) | async-done | bytes 8388624 | tf_op jit(solution)/shard_map/all_gather | solution.py:199
  1030.8 24.3 %multiply_convert_fusion = (bf16[2048,1280]{1,0:T(8,128)(2,1)}, bf16[2048,1280]{1,0:T(8,128)(2,1)}) fusion(f32[2048,1280]{1,0:T(8,128)} %fusion.94, f32[2048,1280]{1,0:T(8,128)} %get-tuple-element.296, bf16[2048,2048]{1,0:T(8,128)(2,1)} %all-gather.9.cloned.1.call-done, bf16[1280,2048]{1,0:T(8,128)(2,1)} %param.33), kind=kOutput, calls=%fused_computation.65 | convolution fusion | flops 10771496960 | bytes 45088768 | tf_op jit(solution)/shard_map/td,fd->tf/dot_general | solution.py:201
  1055.1 17.9 fusion.95
  1073.0 19.2 add_convert_fusion
  1092.3 142.8 %reduce-scatter.9.cloned.1.call-done = bf16[512,2048]{1,0:T(8,128)(2,1)} async-done(((bf16[2048,2048]{1,0:T(8,128)(2,1)}), bf16[512,2048]{1,0:T(8,128)(2,1)}) %reduce-scatter.9.cloned.1.call-update) | async-done | bytes 2097168 | tf_op jit(solution)/shard_map/reduce_scatter | solution.py:208
  1235.1 5.8 fusion.61
  1241.0 6.3 fusion.88
  1250.4 17.0 convolution_convert_fusion.2
  1267.4 15.5 convolution_convert_fusion.3
  1282.9 13.9 convolution_convert_fusion.4
  1296.8 101.0 %all-gather.11.cloned.1.call-done = bf16[2048,2048]{1,0:T(8,128)(2,1)} async-done(((bf16[512,2048]{1,0:T(8,128)(2,1)}), bf16[2048,2048]{1,0:T(8,128)(2,1)}) %all-gather.11.cloned.1.call-update) | async-done | bytes 8388624 | tf_op jit(solution)/shard_map/all_gather | solution.py:219
  1397.8 6.7 convolution_convert_fusion.6
  1404.5 125.9 %while.27 = (s32[]{:T(128)}, f32[2,1024,4,64]{1,0,3,2:T(2,128)}, f32[2,1024,1,64]{1,0,3,2:T(2,128)}, bf16[2,1024,1,64]{1,3,2,0:T(8,128)(2,1)}, bf16[2,1024,1,64]...) while((s32[]{:T(128)}, f32[2,1024,4,64]{1,0,3,2:T(2,128)}, ...), condition=%wide.region_18.19_spmd, body=%wide.region_16.18_spmd.sunk | while | flops 2729767936 | bytes 147803392 | solution.py:226
  1409.2 3.3 fusion.161
  1412.5 10.5 fusion.163
  1423.0 9.1 fusion.167
  1432.1 8.0 fusion.164
  1448.5 18.9 dynamic_update_slice.38
  1471.9 3.3 fusion.161
  1475.2 10.5 fusion.163
  1485.6 9.1 fusion.167
  1494.7 8.0 fusion.164
  1511.2 18.9 dynamic_update_slice.38
  1538.6 3.1 reshape.393
  1548.2 3.5 fusion.76
  1554.5 3.3 convolution_convert_fusion.5
  1559.0 9.3 convolution_convert_fusion
  1572.8 5.8 dynamic_update_slice.26
  1578.8 8.7 dynamic_update_slice.25
  1589.5 197.7 %all-reduce.8.cloned.1.call-done = (bf16[2048,256]{0,1:T(8,128)(2,1)}, bf16[256,2048]{1,0:T(8,128)(2,1)}, bf16[2048,1280]{1,0:T(8,128)(2,1)}, bf16[2048,1280]{1,0:T(8,128)(2,1)}, bf16[1280,2048]{1,0:T(8,128)(2,1)}) async-done(((bf16[2048,256]{0,1:T(8,128)(2,1)}, bf16[256,2048]{1,0:T(8,128)(2,1)}, bf16[2048,1280]{1,0:T(8,128)(2,1)}, bf16[2048,1280]{1,0:T(8,128)(2,1)}, bf16[1280,2048]{1,0:T(8,128)(2,1)}), ...) | async-done | bytes 17825808 | tf_op jit(solution)/shard_map/psum | solution.py:287
  1789.8 2.9 convert_element_type.135
  1792.8 7.5 convert_element_type.137
  1800.3 4.9 convert_element_type.139
  1805.3 5.5 convert_element_type.141
  1810.8 123.4 %reduce-scatter.11.cloned.1.call-done = bf16[512,2048]{1,0:T(8,128)(2,1)} async-done(((bf16[2048,2048]{1,0:T(8,128)(2,1)}), bf16[512,2048]{1,0:T(8,128)(2,1)}) %reduce-scatter.11.cloned.1.call-update) | async-done | bytes 2097168 | tf_op jit(solution)/shard_map/reduce_scatter | solution.py:257
  1934.2 3.2 fusion.68
  1937.3 41.8 %all-reduce = (f32[]{:T(128)}, f32[64]{0:T(128)}, f32[64]{0:T(128)}, f32[2048]{0:T(1024)}, f32[2048]{0:T(1024)}) all-reduce(f32[]{:T(128)} %get-tuple-element.206, f32[64]{0:T(128)S(1)} %reduce_sum.163, f32[64]{0:T(128)S(1)} %get-tuple-element.209, ...), channel_id=1, replica_groups=mesh['dp'=8,'tensor'=4] {'dp','tensor'}, use_global_device_ids=true, to_apply=%region_11.12 | all-reduce | flops 4225 | bytes 33800 | tf_op jit(solution)/shard_map/psum | solution.py:193
  1979.8 6.1 fusion.56
  1986.0 97.6 %all-reduce.6.cloned.1.call-done = (f32[2048,256]{1,0:T(8,128)}, f32[2048,256]{1,0:T(8,128)}) async-done(((f32[2048,256]{1,0:T(8,128)}, f32[2048,256]{1,0:T(8,128)}), (f32[2048,256]{1,0:T(8,128)}, f32[2048,256]{1,0:T(8,128)})) %all-reduce.6.cloned.1.call-update) | async-done | bytes 4194320 | tf_op jit(solution)/shard_map/psum | solution.py:293
  2083.6 3.2 copy.160
  (275 shorter events, 86.9 us)
Async XLA Ops:
  7.2 224.2 %copy-start = (bf16[256,2048]{1,0:T(8,128)(2,1)S(1)}, bf16[256,2048]{1,0:T(8,128)(2,1)}, u32[]{:S(2)}) copy-start(bf16[256,2048]{1,0:T(8,128)(2,1)} %param.28) | copy-start | bytes 3145732
  7.2 159.3 %all-gather.5.cloned.1.call-start = ((), (), s32[]{:S(2)}) async-start(), calls=%async_computation.4 | async-start | bytes 10485760 | tf_op jit(solution)/shard_map/all_gather | solution.py:142
  14.0 505.9 %reduce-scatter.5.cloned.1.call-start = ((), (), s32[]{:S(2)}) async-start(), calls=%async_computation.5 | async-start | bytes 20971520 | tf_op jit(solution)/shard_map/reduce_scatter | solution.py:172
  15.1 163.1 %copy-start.16 = (f32[8,8,2,1024]{3,1,2,0:T(8,128)}, f32[8,8,2,1024]{3,1,2,0:T(8,128)S(1)}, u32[]{:S(2)}) copy-start(f32[8,8,2,1024]{3,1,2,0:T(8,128)S(1)} %copy.112) | copy-start | bytes 1572868
  15.9 162.3 %copy-start.7 = (f32[8,8,2,1024]{3,1,2,0:T(8,128)}, f32[8,8,2,1024]{3,1,2,0:T(8,128)S(1)}, u32[]{:S(2)}) copy-start(f32[8,8,2,1024]{3,1,2,0:T(8,128)S(1)} %copy.111) | copy-start | bytes 1572868
  17.7 156.1 %copy-start.28 = (bf16[2048,64]{1,0:T(8,128)(2,1)}, bf16[2048,64]{1,0:T(8,128)(2,1)S(1)}, u32[]{:S(2)}) copy-start(bf16[2048,64]{1,0:T(8,128)(2,1)S(1)} %get-tuple-element.297) | copy-start | bytes 786436
  17.7 156.1 %copy-start.30 = (bf16[2048,64]{1,0:T(8,128)(2,1)}, bf16[2048,64]{1,0:T(8,128)(2,1)S(1)}, u32[]{:S(2)}) copy-start(bf16[2048,64]{1,0:T(8,128)(2,1)S(1)} %get-tuple-element.298) | copy-start | bytes 786436
  173.8 3.2 copy-start.49
  175.5 4.9 copy-start.45
  176.1 6.2 copy-start.33
  176.7 5.6 copy-start.26
  182.4 7.6 slice-start
  192.7 4.0 copy-start.55
  231.4 9.8 copy-start.10
  231.4 9.9 copy-start.18
  241.3 278.7 %copy-start.3 = (bf16[512,2048]{1,0:T(8,128)(2,1)S(1)}, bf16[512,2048]{1,0:T(8,128)(2,1)}, u32[]{:S(2)}) copy-start(bf16[512,2048]{1,0:T(8,128)(2,1)} %param.19) | copy-start | bytes 6291460
  241.3 284.6 %copy-start.36 = (f32[2048]{0:T(1024)S(1)}, f32[2048]{0:T(1024)}, u32[]{:S(2)}) copy-start(f32[2048]{0:T(1024)} %param.30) | copy-start | bytes 24580
  241.3 439.0 %all-gather.7.cloned.1.call-start = ((), (), s32[]{:S(2)}) async-start(), calls=%async_computation.6 | async-start | bytes 10485760 | tf_op jit(solution)/shard_map/all_gather | solution.py:180
  529.8 345.1 %reduce-scatter.7.cloned.1.call-start = ((), (), s32[]{:S(2)}) async-start(), calls=%async_computation.7 | async-start | bytes 10485760 | tf_op jit(solution)/shard_map/reduce_scatter | solution.py:185
  680.3 16.9 copy-start.54
  731.0 143.9 %copy-start.5 = (bf16[512,2048]{1,0:T(8,128)(2,1)S(1)}, bf16[512,2048]{1,0:T(8,128)(2,1)}, u32[]{:S(2)}) copy-start(bf16[512,2048]{1,0:T(8,128)(2,1)} %param.20) | copy-start | bytes 6291460
  731.0 299.8 %all-gather.9.cloned.1.call-start = ((), (), s32[]{:S(2)}) async-start(), calls=%async_computation.8 | async-start | bytes 10485760 | tf_op jit(solution)/shard_map/all_gather | solution.py:199
  880.3 354.8 %reduce-scatter.9.cloned.1.call-start = ((), (), s32[]{:S(2)}) async-start(), calls=%async_computation.9 | async-start | bytes 10485760 | tf_op jit(solution)/shard_map/reduce_scatter | solution.py:208
  1092.2 142.9 %copy-start.37 = (f32[2048]{0:T(1024)S(1)}, f32[2048]{0:T(1024)}, u32[]{:S(2)}) copy-start(f32[2048]{0:T(1024)} %param.30) | copy-start | bytes 24580
  1092.2 142.9 %copy-start.44 = (f32[512]{0:T(512)S(1)}, f32[512]{0:T(512)}, u32[]{:S(2)}) copy-start(f32[512]{0:T(512)} %copy-done.43) | copy-start | bytes 6148
  1092.2 148.7 %copy-start.48 = (f32[512]{0:T(512)S(1)}, f32[512]{0:T(512)}, u32[]{:S(2)}) copy-start(f32[512]{0:T(512)} %get-tuple-element.289) | copy-start | bytes 6148
  1092.2 305.6 %all-gather.11.cloned.1.call-start = ((), (), s32[]{:S(2)}) async-start(), calls=%async_computation.10 | async-start | bytes 10485760 | tf_op jit(solution)/shard_map/all_gather | solution.py:219
  1235.1 5.8 copy-start.6
  1235.1 5.8 copy-start.12
  1240.9 8.8 copy-start.46
  1247.3 20.1 slice-start.13
  1247.3 540.0 %all-reduce.8.cloned.1.call-start = ((), (), s32[]{:S(2)}) async-start(), calls=%async_computation.13 | async-start | bytes 35651584 | tf_op jit(solution)/shard_map/psum | solution.py:287
  1250.4 17.0 slice-start.14
  1250.4 32.5 %slice-start.9 = ((s8[8388608]{0:T(1024)(128)(4,1)}), s8[4194304]{0:T(1024)(128)(4,1)S(1)}, s32[]{:S(2)}) async-start(s8[8388608]{0:T(1024)(128)(4,1)} %bitcast.333), calls=%async_computation.23 | async-start | bytes 8388608
  1250.4 32.5 %slice-start.11 = ((s8[5242880]{0:T(1024)(128)(4,1)}), s8[4194304]{0:T(1024)(128)(4,1)S(1)}, s32[]{:S(2)}) async-start(s8[5242880]{0:T(1024)(128)(4,1)} %bitcast.335), calls=%async_computation.25 | async-start | bytes 8388608
  1267.4 15.5 slice-start.10
  1267.4 15.5 slice-start.12
  1296.8 107.8 %copy-start.56 = (s32[2]{0:T(128)S(1)}, s32[2]{0:T(128)}, u32[]{:S(2)}) copy-start(s32[2]{0:T(128)} %param.22) | copy-start | bytes 28
  1432.1 8.0 copy-start.11
  1442.7 3.9 copy-start.23
  1448.5 18.9 copy-start.24
  1494.7 8.0 copy-start.11
  1505.4 3.9 copy-start.23
  1511.2 18.9 copy-start.24
  1530.5 5.9 copy-start.8
  1530.5 5.9 copy-start.34
  1530.5 5.9 copy-start.50
  1543.8 3.7 slice-start.7
  1545.4 2.8 slice-start.8
  1546.5 8.0 slice-start.1
  1548.2 6.3 slice-start.2
  1548.2 6.3 copy-start.15
  1557.9 376.3 %reduce-scatter.11.cloned.1.call-start = ((), (), s32[]{:S(2)}) async-start(), calls=%async_computation.11 | async-start | bytes 10485760 | tf_op jit(solution)/shard_map/reduce_scatter | solution.py:257
  1568.3 515.2 %all-reduce.6.cloned.1.call-start = ((), (), s32[]{:S(2)}) async-start(), calls=%async_computation.12 | async-start | bytes 8388608 | tf_op jit(solution)/shard_map/psum | solution.py:293
  1789.8 10.5 slice-start.5
  1792.8 7.5 slice-start.6
  1792.8 12.4 slice-start.3
  1800.3 4.9 slice-start.4
  1805.2 128.9 %copy-start.4 = (bf16[512,2048]{1,0:T(8,128)(2,1)S(1)}, bf16[512,2048]{1,0:T(8,128)(2,1)}, u32[]{:S(2)}) copy-start(bf16[512,2048]{1,0:T(8,128)(2,1)} %param.19) | copy-start | bytes 6291460
  1805.2 128.9 %copy-start.38 = (f32[2048]{0:T(1024)S(1)}, f32[2048]{0:T(1024)}, u32[]{:S(2)}) copy-start(f32[2048]{0:T(1024)} %param.29) | copy-start | bytes 24580
  1805.3 128.9 %copy-start.41 = (f32[512]{0:T(512)S(1)}, f32[512]{0:T(512)}, u32[]{:S(2)}) copy-start(f32[512]{0:T(512)} %copy-done.40) | copy-start | bytes 6148
  1810.8 126.6 %copy-start.42 = (f32[2048]{0:T(1024)S(1)}, f32[2048]{0:T(1024)}, u32[]{:S(2)}) copy-start(f32[2048]{0:T(1024)} %get-tuple-element.204) | copy-start | bytes 24580
  1810.8 169.1 %copy-start.51 = (f32[512]{0:T(512)S(1)}, f32[512]{0:T(512)}, u32[]{:S(2)}) copy-start(f32[512]{0:T(512)} %get-tuple-element.287) | copy-start | bytes 6148
  2083.6 3.2 copy-start.22
  (21 other events, 29.7 us)
Sparse Core Ops, SparseCore 0:
  14.1 152.3 all-gather.4
  241.4 278.5 reduce-scatter.4
  529.9 150.3 all-gather.6
  731.1 143.6 reduce-scatter.6
  880.4 150.3 all-gather.8
  1092.4 142.6 reduce-scatter.8
  1247.4 150.3 all-gather.10
  1558.0 229.2 all-reduce.7
  1789.6 144.4 reduce-scatter.10
  1940.3 143.1 all-reduce.5
where the time goes:
time: 2110 us; the launch traced here: 2100 us
  waiting for transfers between devices  1490 us (71%)
  matrix products  273 us (13%)
  local copies, waits for them, and re-layouts  115 us (5%)
  other arithmetic  113 us (5%)
  blocking collectives  84.9 us (4%)
    reduce_scatter x1, waiting for transfers between devices, body(): lax.psum_scatter(jnp.dot(attended_low, w_out, preferred_element_type=jnp....  279 us
    psum x1, waiting for transfers between devices, body(): lax.psum(grad_query.astype(jnp.bfloat16), 'dp').astype(jnp.float32)  198 us
    all_gather x1, waiting for transfers between devices, body(): normed_two_all = lax.all_gather(normed_two, 'tensor', axis=0, tiled=True)  150 us
    all_gather x1, waiting for transfers between devices, body(): lax.all_gather(cotangent.astype(jnp.bfloat16), 'tensor', axis=0, tiled=True)  150 us
    all_gather x1, waiting for transfers between devices, body(): normed_all = lax.all_gather(normed_input, 'tensor', axis=0, tiled=True)  149 us
    reduce_scatter x1, waiting for transfers between devices, body(): lax.psum_scatter((jnp.einsum('tf,df->td', gate_part, w_gate, preferred_el...  143 us
    reduce_scatter x1, waiting for transfers between devices, body(): lax.psum_scatter(jnp.einsum('tc,dc->td', back_rows, proj_weight, preferre...  123 us
    all_gather x1, waiting for transfers between devices, body(): lax.all_gather(grad_middle.astype(jnp.bfloat16), 'tensor', axis=0, tiled=...  101 us
  transfers between devices with their start and end apart: 10, of which 10 were waited for; matrix products, arithmetic and copies ran while one was open for 5% of the time, Pallas kernels for 0%

commit v1 on v0

v1 whole, which is shorter than its diff:
```python
import jax
import jax.numpy as jnp
from jax import lax
from jax.sharding import PartitionSpec as P

QUERY_HEADS = 16
KEY_VALUE_HEADS = 4
HEAD_SIZE = 64
SEQ_LEN = 1024
GROUP = QUERY_HEADS // KEY_VALUE_HEADS
EPSILON = 1e-06
BF = jnp.bfloat16
F32 = jnp.float32


def rope_rows(start, rows):
    half = HEAD_SIZE // 2
    frequency = 10000.0 ** (-2.0 * jnp.arange(half, dtype=F32) / HEAD_SIZE)
    angles = (start + jnp.arange(rows)).astype(F32)[:, None] * frequency[None, :]
    cosine = jnp.concatenate([jnp.cos(angles), jnp.cos(angles)], 1)
    sine = jnp.concatenate([jnp.sin(angles), jnp.sin(angles)], 1)
    return cosine[:, None, :], sine[:, None, :]


def rotate(vector, cosine, sine):
    half = vector.shape[-1] // 2
    turned = jnp.concatenate([-vector[..., half:], vector[..., :half]], -1)
    return vector * cosine + turned * sine


def unrotate(gradient, cosine, sine):
    half = gradient.shape[-1] // 2
    shifted = gradient * sine
    return gradient * cosine + jnp.concatenate([shifted[..., half:], -shifted[..., :half]], -1)


def inv_root(vector):
    return lax.rsqrt(jnp.mean(vector * vector, axis=-1, keepdims=True) + EPSILON)


def norm_back(gradient, source, factor, gain):
    scaled = gradient * gain
    return factor * scaled - source * factor**3 * jnp.mean(scaled * source, axis=-1, keepdims=True)


def dot(a, b):
    return jnp.dot(a, b, preferred_element_type=F32)


def dot_t(a, b):
    return lax.dot_general(a, b, (((1,), (1,)), ((), ())), preferred_element_type=F32)


def t_dot(a, b):
    return lax.dot_general(a, b, (((0,), (0,)), ((), ())), preferred_element_type=F32)


def seen(start, rows, prefix_len):
    row = start + jnp.arange(rows)[:, None]
    col = jnp.arange(SEQ_LEN)[None, :]
    return (col <= row) | (row < prefix_len) & (col < prefix_len)


def attend(q, k, v, start, prefix_len):
    rows = q.shape[0]
    grouped = q.reshape(rows, KEY_VALUE_HEADS, GROUP, HEAD_SIZE)
    scores = jnp.einsum("ikgd,jkd->kgij", grouped, k, preferred_element_type=F32) * HEAD_SIZE**-0.5
    allowed = seen(start, rows, prefix_len)
    scores = jnp.where(allowed, scores, -1e30)
    top = jnp.max(scores, -1, keepdims=True)
    weights = jnp.where(allowed, jnp.exp(scores - top), 0.0)
    total = jnp.sum(weights, -1, keepdims=True)
    probs = (weights / total).astype(BF)
    attended = jnp.einsum("kgij,jkd->ikgd", probs, v, preferred_element_type=F32)
    return attended.reshape(rows, QUERY_HEADS * HEAD_SIZE), (top + jnp.log(total))[..., 0]


def attend_back(q, k, v, start, prefix_len, lse, grad):
    rows = q.shape[0]
    scale = HEAD_SIZE**-0.5
    grouped = q.reshape(rows, KEY_VALUE_HEADS, GROUP, HEAD_SIZE)
    scores = jnp.einsum("ikgd,jkd->kgij", grouped, k, preferred_element_type=F32) * scale
    allowed = seen(start, rows, prefix_len)
    probs = jnp.where(allowed, jnp.exp(jnp.where(allowed, scores, -1e30) - lse[..., None]), 0.0)
    heads = grad.reshape(rows, KEY_VALUE_HEADS, GROUP, HEAD_SIZE)
    dprobs = jnp.einsum("ikgd,jkd->kgij", heads, v, preferred_element_type=F32)
    inner = jnp.sum(probs * dprobs, -1, keepdims=True)
    dscores = (probs * (dprobs - inner)).astype(BF)
    dq = jnp.einsum("kgij,jkd->ikgd", dscores, k, preferred_element_type=F32) * scale
    dk = jnp.einsum("kgij,ikgd->jkd", dscores, grouped, preferred_element_type=F32) * scale
    dv = jnp.einsum("kgij,ikgd->jkd", probs.astype(BF), heads, preferred_element_type=F32)
    return dq.reshape(rows, QUERY_HEADS, HEAD_SIZE), dk, dv


def sum_small(vector):
    return jnp.sum(lax.all_gather(vector[None], ("dp", "tensor"), axis=0, tiled=True), 0)


def body(
    tokens,
    teacher,
    valid,
    prefix,
    w_query,
    key_weight,
    value_weight,
    query_gain,
    key_gain,
    w_out,
    attn_gain,
    ffn_gain,
    w_gate,
    w_up,
    w_down,
):
    rows, width = tokens.shape
    dp_size, t_size = lax.axis_size("dp"), lax.axis_size("tensor")
    dp_at, t_at = lax.axis_index("dp"), lax.axis_index("tensor")
    per_seq = SEQ_LEN // rows
    seq_groups = [list(range(g, g + per_seq)) for g in range(0, t_size, per_seq)]
    start = t_at % per_seq * rows
    prefix_len = prefix[t_at // per_seq]
    q_all = QUERY_HEADS * HEAD_SIZE
    kv_all = KEY_VALUE_HEADS * HEAD_SIZE
    q_dev = w_query.shape[1]
    cut = width // dp_size

    count = sum_small(jnp.broadcast_to(jnp.sum(valid).astype(F32), (128,)))[0]

    query_cut = lax.dynamic_slice_in_dim(w_query, dp_at * cut, cut, 0)
    query_full = (
        lax.all_gather(query_cut, ("dp", "tensor"), axis=0, tiled=False)
        .reshape(dp_size, t_size, cut, q_dev)
        .transpose(0, 2, 1, 3)
        .reshape(width, q_all)
    )
    out_rows = w_out.shape[0] // dp_size
    out_cut = lax.dynamic_slice_in_dim(w_out, dp_at * out_rows, out_rows, 0)
    out_full = lax.all_gather(out_cut, ("tensor", "dp"), axis=0, tiled=True)

    source = tokens.astype(F32)
    factor_one = inv_root(source)
    normed = (source * factor_one * attn_gain).astype(BF)
    k_raw = dot(normed, key_weight).reshape(rows, KEY_VALUE_HEADS, HEAD_SIZE)
    v_low = dot(normed, value_weight).astype(BF)
    cosine, sine = rope_rows(start, rows)
    k_factor = inv_root(k_raw)
    k_low = rotate(k_raw * k_factor * key_gain, cosine, sine).astype(BF).reshape(rows, kv_all)
    kv_seq = lax.all_gather(
        jnp.concatenate([k_low, v_low], 1),
        "tensor",
        axis=0,
        tiled=True,
        axis_index_groups=seq_groups,
    )
    k_seq = kv_seq[:, :kv_all].reshape(SEQ_LEN, KEY_VALUE_HEADS, HEAD_SIZE)
    v_seq = kv_seq[:, kv_all:].reshape(SEQ_LEN, KEY_VALUE_HEADS, HEAD_SIZE)
    q_raw = dot(normed, query_full).reshape(rows, QUERY_HEADS, HEAD_SIZE)
    q_factor = inv_root(q_raw)
    q_low = rotate(q_raw * q_factor * query_gain, cosine, sine).astype(BF)
    attended, lse = attend(q_low, k_seq, v_seq, start, prefix_len)
    attended = attended.astype(BF)
    middle = source + dot(attended, out_full)

    factor_two = inv_root(middle)
    normed_two = (middle * factor_two * ffn_gain).astype(BF)
    normed_two_all = lax.all_gather(normed_two, "tensor", axis=0, tiled=True)
    gate = dot(normed_two_all, w_gate)
    up = dot(normed_two_all, w_up)
    sig = jax.nn.sigmoid(gate)
    hidden = (gate * sig * up).astype(BF)
    result = middle + lax.psum_scatter(
        dot(hidden, w_down).astype(BF), "tensor", scatter_dimension=0, tiled=True
    ).astype(F32)
    mask = valid.astype(F32)[:, None]
    error = result - teacher.astype(F32)
    squares = jnp.sum(error * error * mask)
    cot = (rows * t_size * dp_size / count) * error * mask
    cot_all = lax.all_gather(cot.astype(BF), "tensor", axis=0, tiled=True)
    grad_down = t_dot(hidden, cot_all)
    dhidden = dot_t(cot_all, w_down)
    dgate = (dhidden * up * sig * (1.0 + gate * (1.0 - sig))).astype(BF)
    dup = (dhidden * gate * sig).astype(BF)
    dn2 = lax.psum_scatter(
        (dot_t(dgate, w_gate) + dot_t(dup, w_up)).astype(BF),
        "tensor",
        scatter_dimension=0,
        tiled=True,
    ).astype(F32)
    grad_gate = t_dot(normed_two_all, dgate)
    grad_up = t_dot(normed_two_all, dup)
    grad_gate, grad_up, grad_down = (
        lax.psum(g.astype(BF), "dp").astype(F32) for g in (grad_gate, grad_up, grad_down)
    )
    grad_ffn_gain = jnp.sum(dn2 * middle * factor_two, 0)
    dmiddle = cot + norm_back(dn2, middle, factor_two, ffn_gain)

    da = dmiddle.astype(BF)
    grad_out_t = t_dot(da, attended).astype(BF)
    dattended = dot_t(da, out_full).astype(BF)
    dq_rot, dk_part, dv_part = attend_back(
        q_low, k_seq, v_seq, start, prefix_len, lse, dattended
    )
    dkv = lax.psum_scatter(
        jnp.concatenate(
            [dk_part.reshape(SEQ_LEN, kv_all), dv_part.reshape(SEQ_LEN, kv_all)], 1
        ).astype(BF),
        "tensor",
        scatter_dimension=0,
        tiled=True,
        axis_index_groups=seq_groups,
    ).astype(F32)
    dq_normed = unrotate(dq_rot, cosine, sine)
    dk_normed = unrotate(
        dkv[:, :kv_all].reshape(rows, KEY_VALUE_HEADS, HEAD_SIZE), cosine, sine
    )
    grad_query_gain = jnp.sum(dq_normed * q_raw * q_factor, (0, 1))
    grad_key_gain = jnp.sum(dk_normed * k_raw * k_factor, (0, 1))
    dq = norm_back(dq_normed, q_raw, q_factor, query_gain).reshape(rows, q_all).astype(BF)
    dk = norm_back(dk_normed, k_raw, k_factor, key_gain).reshape(rows, kv_all).astype(BF)
    dv = dkv[:, kv_all:].astype(BF)
    dn1 = dot_t(dq, query_full) + dot_t(dk, key_weight) + dot_t(dv, value_weight)
    grad_attn_gain = jnp.sum(dn1 * source * factor_one, 0)
    grad_tokens = dmiddle + norm_back(dn1, source, factor_one, attn_gain)
    grad_query = t_dot(normed, dq).astype(BF)
    grad_kv = t_dot(normed, jnp.concatenate([dk, dv], 1)).astype(BF)

    wide = jnp.concatenate([grad_query, grad_out_t, grad_kv], 1)
    wide = lax.psum_scatter(wide, "dp", scatter_dimension=0, tiled=True)
    parts = jnp.concatenate(
        [
            wide[:, : 2 * q_all].reshape(cut, 2, t_size, q_dev).transpose(0, 2, 1, 3).reshape(cut, t_size, 2 * q_dev),
            wide[:, 2 * q_all :].reshape(cut, t_size, 2 * kv_all // t_size),
        ],
        2,
    ).reshape(cut, -1)
    parts = lax.psum_scatter(parts, "tensor", scatter_dimension=1, tiled=True)
    own = lax.all_gather(parts[:, : 2 * q_dev], "dp", axis=0, tiled=True).astype(F32)
    grad_query = own[:, :q_dev]
    grad_out = own[:, q_dev:].T
    kv = (
        lax.all_gather(parts[:, 2 * q_dev :], ("dp", "tensor"), axis=0, tiled=False)
        .reshape(dp_size, t_size, cut, 2 * kv_all // t_size)
        .transpose(0, 2, 1, 3)
        .reshape(width, 2 * kv_all)
        .astype(F32)
    )
    small = sum_small(
        jnp.concatenate(
            [
                grad_attn_gain,
                grad_ffn_gain,
                grad_query_gain,
                grad_key_gain,
                jnp.broadcast_to(squares, (128,)),
            ]
        )
    )
    loss = small[2 * width + 2 * HEAD_SIZE] / (count * width)
    return (
        result.astype(BF),
        loss,
        grad_tokens,
        grad_query,
        kv[:, :kv_all],
        kv[:, kv_all:],
        small[2 * width : 2 * width + HEAD_SIZE],
        small[2 * width + HEAD_SIZE : 2 * width + 2 * HEAD_SIZE],
        grad_out,
        small[:width],
        small[width : 2 * width],
        grad_gate,
        grad_up,
        grad_down,
    )


def solution(mesh):
    rows, cols, whole = P(("dp", "tensor"), None), P(None, "tensor"), P()
    down = P("tensor", None)
    return jax.shard_map(
        body,
        mesh=mesh,
        in_specs=(
            rows, rows, P(("dp", "tensor")), P("dp"), cols, whole, whole, whole, whole,
            down, whole, whole, cols, cols, down,
        ),
        out_specs=(
            rows, whole, rows, cols, whole, whole, whole, whole, down, whole, whole,
            cols, cols, down,
        ),
        check_vma=False,
    )
```

time: 2110 us -> 1520 us (0.72)
  waiting for transfers between devices: 1490 us -> 899 us
  local copies, waits for them, and re-layouts: 115 us -> 60.7 us
  blocking collectives: 84.9 us -> 121 us
    reduce_scatter x4 -> x5, waiting for transfers between devices: 643 us -> 309 us  [the longest x1 142 us: body(): lax.psum_scatter((dot_t(dgate, w_gate) + dot_t(dup, w_up)).astype(BF), 't...]
    all_gather x3 -> x6, waiting for transfers between devices: 400 us -> 233 us  [the longest x1 150 us: body(): cot_all = lax.all_gather(cot.astype(BF), 'tensor', axis=0, tiled=True)]
    psum x2 -> x1, waiting for transfers between devices: 295 us -> 208 us  [body(): lax.psum(g.astype(BF), 'dp').astype(F32)]
    psum x2 -> x0, blocking collectives: 84.9 us -> none  [body(): lax.psum((jnp.sum(valid).astype(jnp.float32), jnp.sum(error_rows * error_...]
    all_gather x0 -> x1, blocking collectives: none -> 78 us  [sum_small(): lax.all_gather(vector[None], ('dp', 'tensor'), axis=0, tiled=True)]
    dynamic_update_slice x14 -> x0, local copies, waits for them, and re-layouts: 60.8 us -> none  [the longest x8 44.2 us: body(): lax.map(lambda packed: attend_back(packed[0], packed[1], packed[2], packe...]
    unnamed x0 -> x1, blocking collectives: none -> 43 us
    concatenate x3 -> x6, other arithmetic: 0.12 us -> 22.3 us  [the longest x1 18 us: body(): wide = jnp.concatenate([grad_query, grad_out_t, grad_kv], 1)]
  transfers between devices with their start and end apart: 10 -> 13, of which waited for: 10 -> 11; matrix products, arithmetic and copies ran while one was open for 5% -> 12% of each run, Pallas kernels for 0% -> 0%
where the time goes in v1:
time: 1520 us
  waiting for transfers between devices  899 us (59%)
  matrix products  289 us (19%)
  other arithmetic  127 us (8%)
  blocking collectives  121 us (8%)
  local copies, waits for them, and re-layouts  60.7 us (4%)
  between operations  17.7 us (1%)
    psum x1, waiting for transfers between devices, body(): lax.psum(g.astype(BF), 'dp').astype(F32)  208 us
    all_gather x1, waiting for transfers between devices, body(): cot_all = lax.all_gather(cot.astype(BF), 'tensor', axis=0, tiled=True)  150 us
    all_gather x1, waiting for transfers between devices, body(): normed_two_all = lax.all_gather(normed_two, 'tensor', axis=0, tiled=True)  148 us
    reduce_scatter x1, waiting for transfers between devices, body(): lax.psum_scatter((dot_t(dgate, w_gate) + dot_t(dup, w_up)).astype(BF), 't...  142 us
    reduce_scatter x1, waiting for transfers between devices, body(): lax.psum_scatter(dot(hidden, w_down).astype(BF), 'tensor', scatter_dimens...  98.7 us
    all_gather x1, blocking collectives, sum_small(): lax.all_gather(vector[None], ('dp', 'tensor'), axis=0, tiled=True)  78 us
    dot_general x7, matrix products, dot_t(): lax.dot_general(a, b, (((1,), (1,)), ((), ())), preferred_element_type=F32)  75.1 us
    all_gather x1, waiting for transfers between devices, body(): lax.all_gather(query_cut, ('dp', 'tensor'), axis=0, tiled=False)  63.4 us
  transfers between devices with their start and end apart: 13, of which 11 were waited for; matrix products, arithmetic and copies ran while one was open for 12% of the time, Pallas kernels for 0%

profile of v1, /device:TPU:0, one launch (start us, length us, event | category | flops | bytes accessed | tf_op | source)
XLA Modules:
  0.0 1515.3 jit_solution(16040654577957878719)
XLA Ops:
  7.3 2.1 fusion.17
  9.9 2.9 multiply_reduce_fusion.6
  17.2 1.6 constant_dynamic-slice_fusion.1
  18.8 1.6 constant_dynamic-slice_fusion
  23.7 17.6 %all-gather.12.cloned.1.call-done = bf16[1024,512]{0,1:T(8,128)(2,1)} async-done(((bf16[512,512]{0,1:T(8,128)(2,1)}), bf16[1024,512]{0,1:T(8,128)(2,1)}) %all-gather.12.cloned.1.call-update) | async-done | bytes 1048592 | tf_op jit(solution)/shard_map/all_gather | solution.py:149
  41.3 2.2 fusion.72
  43.6 63.4 %all-gather.22.cloned.1.call-done = bf16[8192,256]{1,0:T(8,128)(2,1)} async-done(((bf16[256,256]{1,0:T(8,128)(2,1)}), bf16[8192,256]{1,0:T(8,128)(2,1)}) %all-gather.22.cloned.1.call-update) | async-done | bytes 4194320 | tf_op jit(solution)/shard_map/all_gather | solution.py:132
  107.0 8.0 copy.56
  115.0 3.7 copy.73
  118.8 2.5 multiply_reduce_fusion.4
  123.6 13.6 fusion.9
  137.2 14.9 fusion.3
  152.8 16.6 %fusion.33 = bf16[4,64,4,512]{3,1,2,0:T(8,128)(2,1)} fusion(bf16[1024,4,64,1]{0,2,3,1:T(8,128)(2,1)S(1)} %bitcast.229, f32[4,4,512]{2,1,0:T(4,128)S(1)} %fusion.3, f32[4,4,512]{2,1,0:T(4,128)S(1)} %get-tuple-element.123, pred[512,1024]{0,1:T(8,128)(4,1)S(1)} %copy-done.10, f32[4,1024,512,4]{2,1,3,0:T(8,128)} %get-tuple-element.124), kind=kOutput, calls=%fused_computation.80 | convolution fusion | flops 1124597760 | bytes 35717120 | tf_op jit(solution)/shard_map/kgij,jkd->ikgd/dot_general | solution.py:74
  169.4 1.6 all-gather.14.cloned.1.call-done
  171.1 5.2 multiply_reduce_fusion.1
  178.3 1.7 multiply_convert_fusion.3
  180.1 148.3 %all-gather.16.cloned.1.call-done = bf16[2048,2048]{1,0:T(8,128)(2,1)} async-done(((bf16[512,2048]{1,0:T(8,128)(2,1)}), bf16[2048,2048]{1,0:T(8,128)(2,1)}) %all-gather.16.cloned.1.call-update) | async-done | bytes 8388624 | tf_op jit(solution)/shard_map/all_gather | solution.py:167
  328.4 16.7 %fusion.78 = f32[2048,1280]{1,0:T(8,128)} fusion(bf16[2048,2048]{1,0:T(8,128)(2,1)} %all-gather.16.cloned.1.call-done, bf16[2048,1280]{1,0:T(8,128)(2,1)} %param.27), kind=kOutput, calls=%fused_computation.162 | convolution fusion | flops 10737418240 | bytes 24117248 | tf_op jit(solution)/shard_map/dot_general | solution.py:47
  345.1 17.3 %multiply_convert_fusion.2 = (bf16[2048,1280]{1,0:T(8,128)(2,1)}, f32[2048,1280]{1,0:T(8,128)}) fusion(f32[2048,1280]{1,0:T(8,128)} %fusion.78, bf16[2048,2048]{1,0:T(8,128)(2,1)S(1)} %copy-done.77, bf16[2048,1280]{1,0:T(8,128)(2,1)} %param.28), kind=kOutput, calls=%fused_computation.19 | convolution fusion | flops 10753146880 | bytes 39845888 | tf_op jit(solution)/shard_map/dot_general | solution.py:47
  362.3 16.6 %convolution_convert_fusion = bf16[2048,2048]{1,0:T(8,128)(2,1)} fusion(bf16[2048,1280]{1,0:T(8,128)(2,1)} %get-tuple-element.127, bf16[1280,2048]{1,0:T(8,128)(2,1)} %param.29), kind=kOutput, calls=%fused_computation.27 | convolution fusion | flops 10741612544 | bytes 18874368 | tf_op jit(solution)/shard_map/dot_general | solution.py:47
  381.0 43.0 %all-reduce = f32[32]{0:T(128)S(1)} all-reduce(f32[32]{0:T(128)S(1)} %dynamic-update-slice), channel_id=2, replica_groups=mesh['dp'=8,'tensor'=4] {'dp','tensor'}, use_global_device_ids=true, to_apply=%add | all-reduce | flops 32 | bytes 256
  424.1 98.7 %reduce-scatter.6.cloned.1.call-done = bf16[512,2048]{1,0:T(8,128)(2,1)} async-done(((bf16[2048,2048]{1,0:T(8,128)(2,1)}), bf16[512,2048]{1,0:T(8,128)(2,1)}) %reduce-scatter.6.cloned.1.call-update) | async-done | bytes 2097168 | tf_op jit(solution)/shard_map/reduce_scatter | solution.py:172
  522.8 5.4 fusion.26
  528.3 150.5 %all-gather.18.cloned.1.call-done = bf16[2048,2048]{1,0:T(8,128)(2,1)} async-done(((bf16[512,2048]{1,0:T(8,128)(2,1)}), bf16[2048,2048]{1,0:T(8,128)(2,1)}) %all-gather.18.cloned.1.call-update) | async-done | bytes 8388624 | tf_op jit(solution)/shard_map/all_gather | solution.py:179
  678.7 24.3 %multiply_convert_fusion = (bf16[2048,1280]{1,0:T(8,128)(2,1)}, bf16[2048,1280]{1,0:T(8,128)(2,1)}) fusion(f32[2048,1280]{1,0:T(8,128)} %fusion.78, f32[2048,1280]{1,0:T(8,128)} %get-tuple-element.128, bf16[2048,2048]{1,0:T(8,128)(2,1)} %all-gather.18.cloned.1.call-done, bf16[1280,2048]{1,0:T(8,128)(2,1)} %param.29), kind=kOutput, calls=%fused_computation.17 | convolution fusion | flops 10771496960 | bytes 45088768 | tf_op jit(solution)/shard_map/dot_general | solution.py:51
  703.0 17.9 %fusion.79 = f32[2048,2048]{1,0:T(8,128)} fusion(bf16[2048,1280]{1,0:T(8,128)(2,1)} %get-tuple-element.82, bf16[2048,1280]{1,0:T(8,128)(2,1)} %param.27), kind=kOutput, calls=%fused_computation.163 | convolution fusion | flops 10737418240 | bytes 27262976 | tf_op jit(solution)/shard_map/dot_general | solution.py:51
  720.9 19.4 %add_convert_fusion = bf16[2048,2048]{1,0:T(8,128)(2,1)} fusion(f32[2048,2048]{1,0:T(8,128)} %fusion.79, bf16[2048,1280]{1,0:T(8,128)(2,1)} %get-tuple-element.81, bf16[2048,1280]{1,0:T(8,128)(2,1)} %param.28), kind=kOutput, calls=%fused_computation.11 | convolution fusion | flops 10745806848 | bytes 35651584 | tf_op jit(solution)/shard_map/dot_general | solution.py:51
  741.1 142.1 %reduce-scatter.8.cloned.1.call-done = bf16[512,2048]{1,0:T(8,128)(2,1)} async-done(((bf16[2048,2048]{1,0:T(8,128)(2,1)}), bf16[512,2048]{1,0:T(8,128)(2,1)}) %reduce-scatter.8.cloned.1.call-update) | async-done | bytes 2097168 | tf_op jit(solution)/shard_map/reduce_scatter | solution.py:184
  883.2 6.4 fusion.16
  889.6 3.5 fusion.13
  893.2 1.9 copy-done.16
  895.1 3.3 convolution_convert_fusion.7
  900.0 24.3 %fusion = (f32[4,4,512]{2,1,0:T(4,128)S(1)}, f32[4,1024,512,4]{2,1,3,0:T(8,128)}) fusion(f32[4,4,512]{2,1,0:T(4,128)S(1)} %bitcast.233, pred[512,1024]{0,1:T(8,128)(4,1)S(1)} %copy-done.11, f32[4,1024,512,4]{2,1,3,0:T(8,128)} %get-tuple-element.124, bf16[1024,4,64,1]{0,2,3,1:T(8,128)(2,1)S(1)} %bitcast.230, bf16[512,4,4,64]{0,3,2,1:T(8,128)(2,1)S(1)} %bitcast.227), kind=kOutput, calls=%fused_computation.2 | convolution fusion | flops 1124065280 | bytes 69271552 | tf_op jit(solution)/shard_map/ikgd,jkd->kgij/dot_general | solution.py:86
  924.3 15.9 %fusion.39 = bf16[4,64,1024]{2,1,0:T(8,128)(2,1)} fusion(bf16[512,4,4,64]{0,3,2,1:T(8,128)(2,1)S(1)} %bitcast.228, f32[4,4,512]{2,1,0:T(4,128)S(1)} %bitcast.234, pred[512,1024]{0,1:T(8,128)(4,1)S(1)} %copy-done.11, f32[4,1024,512,4]{2,1,3,0:T(8,128)} %get-tuple-element.124), kind=kOutput, calls=%fused_computation.86 | convolution fusion | flops 1115947008 | bytes 35684352 | tf_op jit(solution)/shard_map/kgij,ikgd->jkd/dot_general | solution.py:91
  940.3 28.0 %fusion.2 = bf16[4,4,512,1024]{2,3,1,0:T(8,128)(2,1)} fusion(f32[4,1024,512,4]{2,1,3,0:T(8,128)} %get-tuple-element.130, f32[4,4,512]{2,1,0:T(4,128)S(1)} %get-tuple-element.129, f32[4,4,512]{2,1,0:T(4,128)S(1)} %bitcast.235, pred[512,1024]{0,1:T(8,128)(4,1)S(1)} %copy-done.11, f32[4,1024,512,4]{2,1,3,0:T(8,128)} %get-tuple-element.124), kind=kLoop, calls=%fused_computation.4 | loop fusion | flops 58720256 | bytes 84475904 | tf_op jit(solution)/shard_map/convert_element_type | solution.py:88
  968.3 11.0 fusion.38
  979.3 10.1 convolution_multiply_fusion
  990.6 2.0 bitcast_multiply_fusion.1
  993.5 1.5 multiply_reduce_fusion.2
  996.6 4.5 convolution_convert_fusion.5
  1001.1 4.4 convolution_convert_fusion.4
  1005.4 6.3 reduce-scatter.10.cloned.1.call-done
  1018.7 18.0 %pad_maximum_fusion = bf16[2048,2560]{0,1:T(8,128)(2,1)} fusion(bf16[2048,512]{0,1:T(8,128)(2,1)S(1)} %convolution_convert_fusion.6, bf16[2048,1024]{0,1:T(8,128)(2,1)S(1)} %copy-done.34, bf16[2048,1024]{0,1:T(8,128)(2,1)S(1)} %copy-done.33), kind=kLoop, calls=%fused_computation.16 | loop fusion | flops 31457280 | bytes 20971520 | tf_op jit(solution)/shard_map/concatenate | solution.py:228
  1037.1 16.7 %convolution_convert_fusion.2 = bf16[2048,1280]{1,0:T(8,128)(2,1)} fusion(bf16[2048,2048]{1,0:T(8,128)(2,1)} %all-gather.16.cloned.1.call-done, bf16[2048,1280]{1,0:T(8,128)(2,1)} %get-tuple-element.81), kind=kOutput, calls=%fused_computation.29 | convolution fusion | flops 10740039680 | bytes 18874368 | tf_op jit(solution)/shard_map/dot_general | solution.py:55
  1053.8 17.0 %convolution_convert_fusion.3 = bf16[2048,1280]{1,0:T(8,128)(2,1)} fusion(bf16[2048,2048]{1,0:T(8,128)(2,1)} %all-gather.16.cloned.1.call-done, bf16[2048,1280]{1,0:T(8,128)(2,1)} %get-tuple-element.82), kind=kOutput, calls=%fused_computation.30 | convolution fusion | flops 10740039680 | bytes 18874368 | tf_op jit(solution)/shard_map/dot_general | solution.py:55
  1070.8 47.6 %reduce-scatter.12.cloned.1.call-done = bf16[256,2560]{0,1:T(8,128)(2,1)} async-done(((bf16[2048,2560]{0,1:T(8,128)(2,1)}), bf16[256,2560]{0,1:T(8,128)(2,1)}) %reduce-scatter.12.cloned.1.call-update) | async-done | bytes 1310736 | tf_op jit(solution)/shard_map/reduce_scatter | solution.py:229
  1121.2 16.6 %convolution_convert_fusion.1 = bf16[1280,2048]{1,0:T(8,128)(2,1)} fusion(bf16[2048,1280]{1,0:T(8,128)(2,1)} %get-tuple-element.127, bf16[2048,2048]{1,0:T(8,128)(2,1)} %all-gather.18.cloned.1.call-done), kind=kOutput, calls=%fused_computation.28 | convolution fusion | flops 10740039680 | bytes 18874368 | tf_op jit(solution)/shard_map/dot_general | solution.py:55
  1137.9 14.6 reduce-scatter.14.cloned.1.call-done
  1152.5 1.7 slice.124
  1155.7 208.1 %all-reduce.4.cloned.1.call-done = (bf16[2048,1280]{1,0:T(8,128)(2,1)}, bf16[2048,1280]{1,0:T(8,128)(2,1)}, bf16[1280,2048]{1,0:T(8,128)(2,1)}) async-done(((bf16[2048,1280]{1,0:T(8,128)(2,1)}, bf16[2048,1280]{1,0:T(8,128)(2,1)}, bf16[1280,2048]{1,0:T(8,128)(2,1)}), (bf16[2048,1280]{1,0:T(8,128)(2,1)}, bf16[2048,1280]{1,0:T(8,128)(2,1)}, bf16[1280,2048]{1,0:T(8,128)(2,1)})) %all-reduce.4.cloned.1.call-update) | async-done | bytes 15728656 | tf_op jit(solution)/shard_map/psum | solution.py:193
  1363.8 7.9 convert_element_type.180
  1371.7 4.9 convert_element_type.182
  1376.7 5.5 convert_element_type.184
  1382.2 4.4 fusion.80
  1386.7 2.1 fusion.81
  1389.3 3.7 fusion.25
  1393.7 78.0 %all-gather.3 = f32[32,1,4352]{2,1,0:T(1,128)} all-gather(f32[1,1,4352]{2,1,0:T(1,128)S(1)} %reshape.250), channel_id=4, replica_groups=mesh['dp'=8,'tensor'=4] {'dp','tensor'}, dimensions={0}, use_global_device_ids=true | all-gather | bytes 574464 | tf_op jit(solution)/shard_map/all_gather | solution.py:96
  1475.5 6.6 fusion.24
  1482.1 2.9 slice.125
  1485.0 2.9 copy.64
  1489.9 6.0 reshape.239
  1495.9 6.5 copy.63
  1502.4 2.6 copy.76
  1505.1 2.3 fusion.70
  (254 shorter events, 38.5 us)
Async XLA Ops:
  7.2 7.5 copy-start
  7.2 6.5 copy-start.72
  7.2 34.1 %all-gather.12.cloned.1.call-start = ((), (), s32[]{:S(2)}) async-start(), calls=%async_computation.5 | async-start | bytes 1572864 | tf_op jit(solution)/shard_map/all_gather | solution.py:149
  9.4 5.3 copy-start.5
  9.4 5.3 copy-start.56
  9.9 108.8 %copy-start.62 = (f32[512]{0:T(512)}, f32[512]{0:T(512)S(1)}, u32[]{:S(2)}) copy-start(f32[512]{0:T(512)S(1)} %get-tuple-element.114) | copy-start | bytes 6148
  14.7 5.8 copy-start.78
  16.0 106.7 %copy-start.30 = (f32[512,64]{0,1:T(8,128)}, f32[512,64]{0,1:T(8,128)S(1)}, u32[]{:S(2)}) copy-start(f32[512,64]{0,1:T(8,128)S(1)} %get-tuple-element.132) | copy-start | bytes 393220
  16.0 106.7 %copy-start.35 = (f32[512,64]{0,1:T(8,128)}, f32[512,64]{0,1:T(8,128)S(1)}, u32[]{:S(2)}) copy-start(f32[512,64]{0,1:T(8,128)S(1)} %get-tuple-element.133) | copy-start | bytes 393220
  17.1 89.9 %all-gather.22.cloned.1.call-start = ((), (), s32[]{:S(2)}) async-start(), calls=%async_computation.15 | async-start | bytes 4325376 | tf_op jit(solution)/shard_map/all_gather | solution.py:132
  18.8 152.3 %all-gather.14.cloned.1.call-start = ((), (), s32[]{:S(2)}) async-start(), calls=%async_computation.6 | async-start | bytes 4325376 | tf_op jit(solution)/shard_map/all_gather | solution.py:139
  20.4 307.9 %all-gather.16.cloned.1.call-start = ((), (), s32[]{:S(2)}) async-start(), calls=%async_computation.7 | async-start | bytes 10485760 | tf_op jit(solution)/shard_map/all_gather | solution.py:167
  118.7 3.2 copy-start.68
  123.5 13.7 copy-start.18
  137.2 15.0 copy-start.47
  137.2 15.6 %copy-start.44 = (bf16[1024,256]{0,1:T(8,128)(2,1)S(1)}, bf16[1024,256]{0,1:T(8,128)(2,1)}, u32[]{:S(2)}) copy-start(bf16[1024,256]{0,1:T(8,128)(2,1)} %get-tuple-element.94) | copy-start | bytes 1572868
  171.1 7.2 copy-start.54
  180.0 342.7 %reduce-scatter.6.cloned.1.call-start = ((), (), s32[]{:S(2)}) async-start(), calls=%async_computation.8 | async-start | bytes 10485760 | tf_op jit(solution)/shard_map/reduce_scatter | solution.py:172
  328.4 16.7 %copy-start.77 = (bf16[2048,2048]{1,0:T(8,128)(2,1)S(1)}, bf16[2048,2048]{1,0:T(8,128)(2,1)}, u32[]{:S(2)}) copy-start(bf16[2048,2048]{1,0:T(8,128)(2,1)} %all-gather.16.cloned.1.call-done) | copy-start | bytes 25165828
  378.9 143.9 %copy-start.13 = (bf16[512,2048]{1,0:T(8,128)(2,1)S(1)}, bf16[512,2048]{1,0:T(8,128)(2,1)}, u32[]{:S(2)}) copy-start(bf16[512,2048]{1,0:T(8,128)(2,1)} %param.16) | copy-start | bytes 6291460
  378.9 299.8 %all-gather.18.cloned.1.call-start = ((), (), s32[]{:S(2)}) async-start(), calls=%async_computation.9 | async-start | bytes 10485760 | tf_op jit(solution)/shard_map/all_gather | solution.py:179
  424.0 104.1 %copy-start.79 = (f32[128]{0:T(128)}, f32[128]{0:T(128)S(1)}, u32[]{:S(2)}) copy-start(f32[128]{0:T(128)S(1)} %broadcast_reduce_fusion) | copy-start | bytes 1540
  528.2 355.0 %reduce-scatter.8.cloned.1.call-start = ((), (), s32[]{:S(2)}) async-start(), calls=%async_computation.10 | async-start | bytes 10485760 | tf_op jit(solution)/shard_map/reduce_scatter | solution.py:184
  740.3 142.9 %copy-start.55 = (f32[2048]{0:T(1024)S(1)}, f32[2048]{0:T(1024)}, u32[]{:S(2)}) copy-start(f32[2048]{0:T(1024)} %param.26) | copy-start | bytes 24580
  740.3 142.9 %copy-start.61 = (f32[512]{0:T(512)S(1)}, f32[512]{0:T(512)}, u32[]{:S(2)}) copy-start(f32[512]{0:T(512)} %copy-done.60) | copy-start | bytes 6148
  740.4 271.4 %reduce-scatter.10.cloned.1.call-start = ((), (), s32[]{:S(2)}) async-start(), calls=%async_computation.11 | async-start | bytes 1572864 | tf_op jit(solution)/shard_map/reduce_scatter | solution.py:204
  741.1 148.5 %copy-start.71 = (f32[512]{0:T(512)S(1)}, f32[512]{0:T(512)}, u32[]{:S(2)}) copy-start(f32[512]{0:T(512)} %get-tuple-element.115) | copy-start | bytes 6148
  883.2 6.4 copy-start.2
  883.2 6.4 copy-start.14
  883.2 6.4 copy-start.24
  889.6 5.5 copy-start.32
  895.1 4.8 copy-start.11
  895.1 4.8 copy-start.45
  940.2 28.1 %copy-start.19 = (bf16[512,16,64]{0,2,1:T(8,128)(2,1)S(1)}, bf16[512,16,64]{0,2,1:T(8,128)(2,1)}, u32[]{:S(2)}) copy-start(bf16[512,16,64]{0,2,1:T(8,128)(2,1)} %copy-done.18) | copy-start | bytes 3145732
  968.3 11.0 copy-start.29
  979.3 10.2 copy-start.46
  979.3 11.3 copy-start.36
  990.6 127.8 %reduce-scatter.12.cloned.1.call-start = ((), (), s32[]{:S(2)}) async-start(), calls=%async_computation.12 | async-start | bytes 11796480 | tf_op jit(solution)/shard_map/reduce_scatter | solution.py:229
  990.6 2.8 copy-start.12
  995.8 5.3 copy-start.25
  996.6 4.5 copy-start.17
  996.6 4.5 copy-start.39
  1001.1 11.9 copy-start.73
  1005.4 8.9 copy-start.50
  1005.4 9.8 copy-start.7
  1011.7 2.7 copy-start.58
  1011.7 2.7 copy-start.67
  1011.7 3.5 copy-start.64
  1015.2 3.5 copy-start.34
  1036.7 115.8 %reduce-scatter.14.cloned.1.call-start = ((), (), s32[]{:S(2)}) async-start(), calls=%async_computation.13 | async-start | bytes 1638400 | tf_op jit(solution)/shard_map/reduce_scatter | solution.py:237
  1121.0 242.8 %all-reduce.4.cloned.1.call-start = ((), (), s32[]{:S(2)}) async-start(), calls=%async_computation.17 | async-start | bytes 31457280 | tf_op jit(solution)/shard_map/psum | solution.py:193
  1137.8 17.9 %copy-start.80 = (f32[128]{0:T(128)S(1)}, f32[128]{0:T(128)}, u32[]{:S(2)}) copy-start(f32[128]{0:T(128)} %copy-done.79) | copy-start | bytes 1540
  1137.8 344.3 %all-gather.20.cloned.1.call-start = ((), (), s32[]{:S(2)}) async-start(), calls=%async_computation.14 | async-start | bytes 2359296 | tf_op jit(solution)/shard_map/all_gather | solution.py:238
  1154.1 335.7 %all-gather.24.cloned.1.call-start = ((), (), s32[]{:S(2)}) async-start(), calls=%async_computation.16 | async-start | bytes 2162688 | tf_op jit(solution)/shard_map/all_gather | solution.py:242
  1363.8 8.0 copy-start.27
  1363.8 12.9 slice-start
  1371.7 4.9 slice-start.1
  1376.7 5.5 copy-start.9
  1376.7 5.5 copy-start.26
  1382.2 4.4 copy-start.74
  1389.3 4.3 copy-start.59
  1389.3 4.3 copy-start.75
  1389.3 86.2 %copy-start.70 = (f32[512]{0:T(512)S(1)}, f32[512]{0:T(512)}, u32[]{:S(2)}) copy-start(f32[512]{0:T(512)} %get-tuple-element.113) | copy-start | bytes 6148
  1482.1 5.8 copy-start.20
  (33 other events, 57.1 us)
Sparse Core Ops, SparseCore 0:
  17.3 24.0 all-gather.11
  44.9 62.0 all-gather.21
  110.4 60.5 all-gather.13
  180.2 148.1 all-gather.15
  379.0 143.7 reduce-scatter.5
  528.3 150.3 all-gather.17
  740.5 142.6 reduce-scatter.7
  990.6 21.0 reduce-scatter.9
  1036.8 81.5 reduce-scatter.11
  1121.2 31.1 reduce-scatter.13
  1157.5 206.2 all-reduce.3
  1366.1 28.3 all-gather.19
  1397.9 58.5 all-gather.23
